TPU v7x, 32 devices: a whole 2x2x4 slice. The times are simulated.
32 devices in a mesh: phase: 2 (over core), tok: 4 (over z), mp: 4 (over y, x).
Axes of the slice: x: 2, y: 2, z: 4, core: 2. Of those that a mesh axis runs over, the one named last changes fastest.
Arguments:
- hidden: bfloat16 [2, 512, 6656], P('phase', 'tok', 'mp'), may hold values from -30 to 30
- w_qkv: bfloat16 [2, 6656, 3, 4096], P('phase', 'mp', None, 'tok'), may hold values from -1 to 1
- segment_ids: int32 [2, 512], P('phase'), may hold values from 0 to 3, never falling along the last dimension, each value on 1 to 256 neighbouring positions
- exit_flags: int32 [2, 4], P('phase'), may hold values from 0 to 1, as said below
Outputs:
- attended: bfloat16 [2, 512, 4096], P('phase', 'mp', 'tok')
- handed: bfloat16 [2, 512, 4096], P('phase', 'mp', 'tok')
Inputs may be any that keep to these rules, and one draw needn't show every extreme that they name: `exit_flags`: in each micro-batch exactly 2 of the 4 blocks have flag 0.
All inputs are finite; a program needn't handle non-finite values.
Results may differ from a plain program's by a relative error of at most 0.0068.
Values may be sent and summed in bfloat16 or wider, within the bound.
A program may use at most 64 MiB of HBM per device.

v0:
```python
import math
import jax
import jax.numpy as jnp
from jax import lax
from jax.sharding import PartitionSpec as P

HEAD = 128
BLOCK = 128


def shifted(block, axis, distance):
    devices = range(lax.axis_size(axis))
    route = [((i - distance) % len(devices), i) for i in devices]
    return lax.ppermute(block, axis, route)


def attend(query, keys, values, query_pos, segment, key_pos):
    heads_here = query.shape[1] // HEAD
    total = keys.shape[0]
    key_heads = keys.reshape(total, heads_here, HEAD)
    value_heads = values.reshape(total, heads_here, HEAD)
    key_segment = jnp.take(segment, key_pos)
    scale = 1.0 / math.sqrt(HEAD)
    block_rows = query.shape[0]
    scores = (
        jnp.einsum(
            "rhd,shd->hrs",
            query.reshape(block_rows, heads_here, HEAD),
            key_heads,
            preferred_element_type=jnp.float32,
        )
        * scale
    )
    own_segment = jnp.take(segment, query_pos)
    allowed = (key_pos[None, :] <= query_pos[:, None]) & (
        key_segment[None, :] == own_segment[:, None]
    )
    scores = jnp.where(allowed[None], scores, -1e30)
    peak = jnp.max(scores, axis=-1, keepdims=True)
    expo = jnp.exp(scores - peak)
    probs = (expo / jnp.sum(expo, axis=-1, keepdims=True)).astype(jnp.bfloat16)
    mixed = jnp.einsum("hrs,shd->rhd", probs, value_heads, preferred_element_type=jnp.float32)
    return mixed.reshape(block_rows, heads_here * HEAD).astype(jnp.bfloat16)


def local(hidden, w_qkv, segment_ids, exit_flags):
    rows_here = hidden[0]
    weights = w_qkv[0]
    width_here = rows_here.shape[1]
    head_cols = weights.shape[2]
    flat_weights = weights.reshape(width_here, 3 * head_cols)
    segment = segment_ids[0]
    flags = exit_flags[0]
    groups = lax.axis_size("mp")
    member = lax.axis_index("mp")
    partial_value = jnp.dot(
        lax.all_gather(rows_here, "tok", axis=0, tiled=True),
        flat_weights,
        preferred_element_type=jnp.float32,
    )
    total = partial_value.shape[0]
    quarter = total // groups
    query_part = partial_value[:, :head_cols]
    key_value_part = partial_value[:, head_cols:]
    my_pos = member * quarter + jnp.arange(quarter, dtype=jnp.int32)
    my_blocks = my_pos // BLOCK
    alive = jnp.take(flags, my_blocks) == 0
    query = lax.psum_scatter(query_part, "mp", scatter_dimension=0, tiled=True).astype(jnp.bfloat16)
    mine = lax.psum_scatter(key_value_part, "mp", scatter_dimension=0, tiled=True).astype(
        jnp.bfloat16
    )
    key_value = lax.all_gather(mine, "mp", axis=0, tiled=True)
    all_pos = jnp.arange(total, dtype=jnp.int32)
    mixed = attend(
        query, key_value[:, :head_cols], key_value[:, head_cols:], my_pos, segment, all_pos
    )
    zeros = jnp.zeros((quarter, head_cols), jnp.bfloat16)
    result = jnp.where(alive[:, None], mixed, zeros)
    handed = shifted(result, "phase", 1)
    return (result[None], handed[None])


def solution(mesh):
    in_specs = (
        P("phase", "tok", "mp"),
        P("phase", "mp", None, "tok"),
        P("phase", None),
        P("phase", None),
    )
    out_specs = (P("phase", "mp", "tok"), P("phase", "mp", "tok"))
    return jax.shard_map(local, mesh=mesh, in_specs=in_specs, out_specs=out_specs, check_vma=False)
```

profile of v0, /device:TPU:0, one launch (start us, length us, event | category | flops | bytes accessed | tf_op | source)
XLA Modules:
  0.0 207.5 jit_solution(11496909522336261351)
XLA Ops:
  7.2 0.0 all-gather.6.cloned.1.call-start
  7.2 0.7 all-gather.6.cloned.1.call-update
  7.9 0.0 reduce-scatter.3.cloned.1.call-start
  8.0 13.5 %copy.11 = bf16[1,1664,3,1024]{1,3,2,0:T(8,128)(2,1)} copy(bf16[1,1664,3,1024]{3,1,2,0:T(8,128)(2,1)} %param.5) | data formatting | bytes 20447232 | tf_op args[1]
  21.5 30.0 %all-gather.6.cloned.1.call-done = bf16[1,512,1664]{2,1,0:T(8,128)(2,1)} async-done(((bf16[1,128,1664]{2,1,0:T(8,128)(2,1)}), bf16[1,512,1664]{2,1,0:T(8,128)(2,1)}) %all-gather.6.cloned.1.call-update) | async-done | bytes 1703952 | tf_op jit(solution)/shard_map/all_gather | solution.py:57
  51.5 9.1 %fusion.2 = f32[512,3072]{1,0:T(8,128)S(1)} fusion(bf16[1664,3072]{0,1:T(8,128)(2,1)} %bitcast.57, bf16[1,512,1664]{2,1,0:T(8,128)(2,1)} %all-gather.6.cloned.1.call-done), kind=kOutput, calls=%fused_computation.7 | convolution fusion | flops 5234491392 | bytes 18219008 | tf_op jit(solution)/shard_map/dot_general | solution.py:56
  60.6 2.7 %copy-done.1 = f32[512,3072]{1,0:T(8,128)} copy-done((f32[512,3072]{1,0:T(8,128)}, f32[512,3072]{1,0:T(8,128)S(1)}, u32[]{:S(2)}) %copy-start.1) | copy-done | bytes 6291480
  63.3 2.5 %slice.30 = f32[512,2048]{1,0:T(8,128)} slice(f32[512,3072]{1,0:T(8,128)S(1)} %fusion.2), slice={[0:512], [1024:3072]} | slice | bytes 8388608 | tf_op jit(solution)/shard_map/slice | solution.py:64
  65.8 0.0 reduce-scatter.3.cloned.1.call-update
  65.8 0.0 all-gather.4.cloned.1.call-start
  65.9 51.5 %reduce-scatter.3.cloned.1.call-done = f32[128,2048]{1,0:T(8,128)} async-done(((f32[512,2048]{1,0:T(8,128)}), f32[128,2048]{1,0:T(8,128)}) %reduce-scatter.3.cloned.1.call-update) | async-done | bytes 1048592 | tf_op jit(solution)/shard_map/reduce_scatter | solution.py:69
  117.4 2.1 %convert_element_type.29 = bf16[128,2048]{1,0:T(8,128)(2,1)} convert(f32[128,2048]{1,0:T(8,128)} %reduce-scatter.3.cloned.1.call-done) | non-fusion elementwise | flops 262144 | bytes 1572864 | tf_op jit(solution)/shard_map/convert_element_type | solution.py:69
  119.5 0.0 reduce-scatter.5.cloned.1.call-start
  119.6 3.2 %slice.32 = f32[512,1024]{1,0:T(8,128)} slice(f32[512,3072]{1,0:T(8,128)} %copy-done.1), slice={[0:512], [0:1024]} | slice | bytes 4194304 | tf_op jit(solution)/shard_map/slice | solution.py:63
  122.8 3.5 %gather_fusion = s32[512]{0:T(512)S(1)} fusion(s32[512]{0:T(512)S(1)} %bitcast.55, s32[1024]{0:T(1024)S(1)} %pad_clamp_fusion.1), kind=kCustom, calls=%fused_computation | custom fusion | bytes 6144 | tf_op jit(solution)/shard_map/jit(_take)/gather | solution.py:22
  126.4 1.3 gather_fusion.1
  127.7 0.7 fusion.31
  128.3 2.6 %fusion.28 = pred[128]{0:T(512)(128)(4,1)S(1)} fusion(s32[]{:T(128)} %bitcast, s32[]{:T(128)} %bitcast.1, s32[]{:T(128)} %bitcast.3, s32[]{:T(128)} %bitcast.2, s32[]{:T(128)S(6)} %mul.9), kind=kLoop, calls=%fused_computation.48 | loop fusion | flops 6272 | bytes 148 | tf_op jit(solution)/shard_map/eq | solution.py:67
  130.9 0.1 fusion.12
  131.0 23.8 %all-gather.4.cloned.1.call-done = bf16[512,2048]{1,0:T(8,128)(2,1)} async-done(((bf16[128,2048]{1,0:T(8,128)(2,1)}), bf16[512,2048]{1,0:T(8,128)(2,1)}) %all-gather.4.cloned.1.call-update) | async-done | bytes 2097168 | tf_op jit(solution)/shard_map/all_gather | solution.py:72
  154.9 1.7 slice_bitcast_fusion
  156.6 0.5 copy.17
  157.2 35.7 %reduce-scatter.5.cloned.1.call-done = f32[128,1024]{1,0:T(8,128)} async-done(((f32[512,1024]{1,0:T(8,128)}), f32[128,1024]{1,0:T(8,128)}) %reduce-scatter.5.cloned.1.call-update) | async-done | bytes 524304 | tf_op jit(solution)/shard_map/reduce_scatter | solution.py:68
  192.9 3.3 %fusion.32 = (f32[8,128]{1,0:T(8,128)S(1)}, f32[8,128,512]{2,1,0:T(8,128)}) fusion(pred[128,512]{1,0:T(8,128)(4,1)S(1)} %fusion.12, bf16[64,8,8,128]{3,2,1,0:T(8,128)(2,1)S(1)} %get-tuple-element.2, f32[128,1024]{1,0:T(8,128)} %reduce-scatter.5.cloned.1.call-done), kind=kOutput, calls=%fused_computation.53 | convolution fusion | flops 136446464 | bytes 3739648 | tf_op jit(solution)/shard_map/sub | solution.py:40
  196.2 2.2 %convolution_convert_fusion = bf16[8,128,128]{2,1,0:T(8,128)(2,1)S(1)} fusion(bf16[512,8,128]{0,2,1:T(8,128)(2,1)S(1)} %bitcast.58, f32[8,128,512]{2,1,0:T(8,128)} %get-tuple-element.9, f32[8,128]{1,0:T(8,128)S(1)} %get-tuple-element.8), kind=kOutput, calls=%fused_computation.9 | convolution fusion | flops 135397376 | bytes 3411968 | tf_op jit(solution)/shard_map/hrs,shd->rhd/dot_general | solution.py:42
  198.4 0.1 copy.16
  198.6 0.1 broadcast_select_fusion
  198.6 0.1 collective-permute-start
  198.7 0.1 copy.15
  198.9 0.8 broadcast_select_fusion.1
  199.7 0.6 collective-permute-done
  200.2 0.7 copy.45
  (13 shorter events, 0.1 us)
Async XLA Ops:
  7.2 115.7 %copy-start = (s32[1,512]{1,0:T(1,128)S(1)}, s32[1,512]{1,0:T(1,128)}, u32[]{:S(2)}) copy-start(s32[1,512]{1,0:T(1,128)} %param.6) | copy-start | bytes 6148
  7.2 44.3 %all-gather.6.cloned.1.call-start = ((), (), s32[]{:S(2)}) async-start(), calls=%async_computation.5 | async-start | bytes 2129920 | tf_op jit(solution)/shard_map/all_gather | solution.py:57
  7.9 109.5 %reduce-scatter.3.cloned.1.call-start = ((), (), s32[]{:S(2)}) async-start(), calls=%async_computation.2 | async-start | bytes 5242880 | tf_op jit(solution)/shard_map/reduce_scatter | solution.py:69
  60.6 2.7 %copy-start.1 = (f32[512,3072]{1,0:T(8,128)}, f32[512,3072]{1,0:T(8,128)S(1)}, u32[]{:S(2)}) copy-start(f32[512,3072]{1,0:T(8,128)S(1)} %fusion.2) | copy-start | bytes 18874372
  65.8 89.1 %all-gather.4.cloned.1.call-start = ((), (), s32[]{:S(2)}) async-start(), calls=%async_computation.3 | async-start | bytes 2621440 | tf_op jit(solution)/shard_map/all_gather | solution.py:72
  119.5 73.4 %reduce-scatter.5.cloned.1.call-start = ((), (), s32[]{:S(2)}) async-start(), calls=%async_computation.4 | async-start | bytes 2621440 | tf_op jit(solution)/shard_map/reduce_scatter | solution.py:68
  122.8 4.9 %copy-start.2 = (s32[1,4]{1,0:T(1,128)S(1)}, s32[1,4]{1,0:T(1,128)}, u32[]{:S(2)}) copy-start(s32[1,4]{1,0:T(1,128)} %param.7) | copy-start | bytes 52
  198.6 1.6 collective-permute-start
Sparse Core Ops, SparseCore 0:
  9.6 41.8 all-gather.5
  65.9 51.4 reduce-scatter.2
  119.6 35.1 all-gather.3
  157.7 35.1 reduce-scatter.4
where the time goes:
time: 208 us; the launch traced here: 207 us
  waiting for transfers between devices  142 us (68%)
  local copies, waits for them, and re-layouts  30.7 us (15%)
  matrix products  14.6 us (7%)
  between operations  13.9 us (7%)
  other arithmetic  5.68 us (3%)
    reduce_scatter x1, waiting for transfers between devices, local(): lax.psum_scatter(key_value_part, 'mp', scatter_dimension=0, tiled=True)  51.5 us
    reduce_scatter x1, waiting for transfers between devices, local(): lax.psum_scatter(query_part, 'mp', scatter_dimension=0, tiled=True)  35.7 us
    all_gather x1, waiting for transfers between devices, local(): lax.all_gather(rows_here, 'tok', axis=0, tiled=True)  30 us
    all_gather x1, waiting for transfers between devices, local(): key_value = lax.all_gather(mine, 'mp', axis=0, tiled=True)  23.8 us
    unnamed x9, local copies, waits for them, and re-layouts  18.7 us
    dot_general x1, matrix products, local(): jnp.dot(lax.all_gather(rows_here, 'tok', axis=0, tiled=True), flat_weight...  9.08 us
  transfers between devices with their start and end apart: 5, of which 5 were waited for; matrix products, arithmetic and copies ran while one was open for 14% of the time, Pallas kernels for 0%

commit v1 on v0

--- a/solution.py
+++ b/solution.py
@@ -3,9 +3,35 @@
 import jax.numpy as jnp
 from jax import lax
 from jax.sharding import PartitionSpec as P
+from jax.lax import axis_index, ppermute, psum
 
 HEAD = 128
 BLOCK = 128
+
+
+def ticks_fit(z, array_axis):
+    z = jnp.moveaxis(z, 0, array_axis)
+    before = z.shape
+    return z.reshape(
+        *before[:array_axis], before[array_axis] * before[array_axis + 1], *before[array_axis + 2 :]
+    )
+
+
+def save_weights(unit, lane_axis):
+    vec_out = psum(1, axis_name=lane_axis)
+    q_next = axis_index(lane_axis)
+    z1, part_now = (vec_out, q_next)
+    inter, local_out = (unit[None], 1)
+    while local_out < z1:
+        outcome_arr = ppermute(
+            inter, axis_name=lane_axis, perm=[(tick, tick ^ local_out) for tick in range(z1)]
+        )
+        block_now = part_now & local_out == 0
+        inter = jnp.concatenate(
+            [jnp.where(block_now, inter, outcome_arr), jnp.where(block_now, outcome_arr, inter)]
+        )
+        local_out *= 2
+    return inter
 
 
 def shifted(block, axis, distance):
@@ -69,7 +95,7 @@
     mine = lax.psum_scatter(key_value_part, "mp", scatter_dimension=0, tiled=True).astype(
         jnp.bfloat16
     )
-    key_value = lax.all_gather(mine, "mp", axis=0, tiled=True)
+    key_value = ticks_fit(save_weights(mine, "mp"), 0)
     all_pos = jnp.arange(total, dtype=jnp.int32)
     mixed = attend(
         query, key_value[:, :head_cols], key_value[:, head_cols:], my_pos, segment, all_pos

time: 208 us -> 185 us (0.89)
  waiting for transfers between devices: 142 us -> 118 us
  starting transfers between devices: 0.23 us -> 3.08 us
    ppermute x0 -> x2, waiting for transfers between devices: none -> 38.5 us  [save_weights(): ppermute(inter, axis_name=lane_axis, perm=[(tick, tick ^ local_out) for t...]
    reduce_scatter x1, waiting for transfers between devices: 35.7 us -> 0.02 us  [local(): lax.psum_scatter(query_part, 'mp', scatter_dimension=0, tiled=True)]
    all_gather x1 -> x0, waiting for transfers between devices: 23.8 us -> none  [local(): key_value = lax.all_gather(mine, 'mp', axis=0, tiled=True)]
    reduce_scatter x1, waiting for transfers between devices: 51.5 us -> 48.3 us  [local(): lax.psum_scatter(key_value_part, 'mp', scatter_dimension=0, tiled=True)]
    ppermute x0 -> x2, starting transfers between devices: none -> 2.89 us  [save_weights(): ppermute(inter, axis_name=lane_axis, perm=[(tick, tick ^ local_out) for t...]
    convert_element_type x1 -> x0, other arithmetic: 2.09 us -> none  [local(): lax.psum_scatter(key_value_part, 'mp', scatter_dimension=0, tiled=True)]
    unnamed x9 -> x11, local copies, waits for them, and re-layouts: 18.7 us -> 17.2 us
  transfers between devices with their start and end apart: 5 -> 6, of which waited for: 5 -> 5; matrix products, arithmetic and copies ran while one was open for 14% -> 16% of each run, Pallas kernels for 0% -> 0%
where the time goes in v1:
time: 185 us
  waiting for transfers between devices  118 us (64%)
  local copies, waits for them, and re-layouts  29.3 us (16%)
  matrix products  14.5 us (8%)
  between operations  14 us (8%)
  other arithmetic  5.49 us (3%)
  starting transfers between devices  3.08 us (2%)
    reduce_scatter x1, waiting for transfers between devices, local(): lax.psum_scatter(key_value_part, 'mp', scatter_dimension=0, tiled=True)  48.3 us
    ppermute x2, waiting for transfers between devices, save_weights(): ppermute(inter, axis_name=lane_axis, perm=[(tick, tick ^ local_out) for t...  38.5 us
    all_gather x1, waiting for transfers between devices, local(): lax.all_gather(rows_here, 'tok', axis=0, tiled=True)  30.2 us
    unnamed x11, local copies, waits for them, and re-layouts  17.2 us
    dot_general x1, matrix products, local(): jnp.dot(lax.all_gather(rows_here, 'tok', axis=0, tiled=True), flat_weight...  9.08 us
  transfers between devices with their start and end apart: 6, of which 5 were waited for; matrix products, arithmetic and copies ran while one was open for 16% of the time, Pallas kernels for 0%

profile of v1, /device:TPU:0, one launch (start us, length us, event | category | flops | bytes accessed | tf_op | source)
XLA Modules:
  0.0 184.8 jit_solution(17251621786394190999)
XLA Ops:
  7.2 0.7 all-gather.3.cloned.1.call-update
  8.0 13.3 %copy.10 = bf16[1,1664,3,1024]{1,3,2,0:T(8,128)(2,1)} copy(bf16[1,1664,3,1024]{3,1,2,0:T(8,128)(2,1)} %param.5) | data formatting | bytes 20447232 | tf_op args[1]
  21.2 30.2 %all-gather.3.cloned.1.call-done = bf16[1,512,1664]{2,1,0:T(8,128)(2,1)} async-done(((bf16[1,128,1664]{2,1,0:T(8,128)(2,1)}), bf16[1,512,1664]{2,1,0:T(8,128)(2,1)}) %all-gather.3.cloned.1.call-update) | async-done | bytes 1703952 | tf_op jit(solution)/shard_map/all_gather | solution.py:83
  51.5 9.1 %fusion.2 = f32[512,3072]{1,0:T(8,128)S(1)} fusion(bf16[1664,3072]{0,1:T(8,128)(2,1)} %bitcast.51, bf16[1,512,1664]{2,1,0:T(8,128)(2,1)} %all-gather.3.cloned.1.call-done), kind=kOutput, calls=%fused_computation.8 | convolution fusion | flops 5234491392 | bytes 18219008 | tf_op jit(solution)/shard_map/dot_general | solution.py:82
  60.6 2.7 %copy-done.1 = f32[512,3072]{1,0:T(8,128)} copy-done((f32[512,3072]{1,0:T(8,128)}, f32[512,3072]{1,0:T(8,128)S(1)}, u32[]{:S(2)}) %copy-start.1) | copy-done | bytes 6291480
  63.2 2.5 %slice.30 = f32[512,2048]{1,0:T(8,128)} slice(f32[512,3072]{1,0:T(8,128)S(1)} %fusion.2), slice={[0:512], [1024:3072]} | slice | bytes 8388608 | tf_op jit(solution)/shard_map/slice | solution.py:90
  65.8 3.2 %slice.32 = f32[512,1024]{1,0:T(8,128)} slice(f32[512,3072]{1,0:T(8,128)} %copy-done.1), slice={[0:512], [0:1024]} | slice | bytes 4194304 | tf_op jit(solution)/shard_map/slice | solution.py:89
  69.0 48.3 %reduce-scatter.3.cloned.1.call-done = f32[128,2048]{1,0:T(8,128)} async-done(((f32[512,2048]{1,0:T(8,128)}), f32[128,2048]{1,0:T(8,128)}) %reduce-scatter.3.cloned.1.call-update) | async-done | bytes 1048592 | tf_op jit(solution)/shard_map/reduce_scatter | solution.py:95
  117.4 1.4 convert_bitcast_fusion
  118.8 1.5 collective-permute-start
  120.3 16.9 %collective-permute-done = bf16[1,128,2048]{2,1,0:T(8,128)(2,1)S(1)} collective-permute-done((bf16[1,128,2048]{2,1,0:T(8,128)(2,1)S(1)}, bf16[1,128,2048]{2,1,0:T(8,128)(2,1)S(1)}, u32[]{:S(2)}, u32[]{:S(2)}) %collective-permute-start) | collective-permute-done | bytes 524320 | tf_op jit(solution)/shard_map/ppermute | solution.py:26
  137.2 0.1 broadcast_select_fusion.3
  137.3 0.1 pad_maximum_fusion.1
  137.4 1.4 collective-permute-start.1
  138.7 1.3 gather_fusion.1
  140.0 3.5 %gather_fusion = s32[512]{0:T(512)S(1)} fusion(s32[512]{0:T(512)S(1)} %bitcast.49, s32[1024]{0:T(1024)S(1)} %pad_clamp_fusion.1), kind=kCustom, calls=%fused_computation | custom fusion | bytes 6144 | tf_op jit(solution)/shard_map/jit(_take)/gather | solution.py:48
  143.6 0.6 fusion.24
  144.2 2.6 %fusion.20 = pred[128]{0:T(512)(128)(4,1)S(1)} fusion(s32[]{:T(128)} %bitcast, s32[]{:T(128)} %bitcast.1, s32[]{:T(128)} %bitcast.3, s32[]{:T(128)} %bitcast.2, s32[]{:T(128)S(6)} %mul.9), kind=kLoop, calls=%fused_computation.52 | loop fusion | flops 6272 | bytes 148 | tf_op jit(solution)/shard_map/eq | solution.py:93
  146.8 0.1 fusion.10
  146.9 21.7 %collective-permute-done.1 = bf16[2,128,2048]{2,1,0:T(8,128)(2,1)S(1)} collective-permute-done((bf16[2,128,2048]{2,1,0:T(8,128)(2,1)S(1)}, bf16[2,128,2048]{2,1,0:T(8,128)(2,1)S(1)}, u32[]{:S(2)}, u32[]{:S(2)}) %collective-permute-start.1) | collective-permute-done | bytes 1048608 | tf_op jit(solution)/shard_map/ppermute | solution.py:26
  168.6 0.1 broadcast_select_fusion.1
  168.7 0.2 pad_maximum_fusion
  168.9 0.2 fusion.23
  169.1 0.5 copy.18
  169.7 0.5 copy.11
  170.3 3.2 %fusion.25 = (f32[8,128]{1,0:T(8,128)S(1)}, f32[8,128,512]{2,1,0:T(8,128)}) fusion(pred[128,512]{1,0:T(8,128)(4,1)S(1)} %fusion.10, bf16[512,8,128]{0,2,1:T(8,128)(2,1)S(1)} %bitcast.53, f32[128,1024]{1,0:T(8,128)} %reduce-scatter.5.cloned.1.call-done), kind=kOutput, calls=%fused_computation.58 | convolution fusion | flops 136446464 | bytes 3739648 | tf_op jit(solution)/shard_map/sub | solution.py:66
  173.5 2.2 %convolution_convert_fusion = bf16[8,128,128]{2,1,0:T(8,128)(2,1)S(1)} fusion(bf16[512,8,128]{0,2,1:T(8,128)(2,1)S(1)} %bitcast.54, f32[8,128,512]{2,1,0:T(8,128)} %get-tuple-element.13, f32[8,128]{1,0:T(8,128)S(1)} %get-tuple-element.12), kind=kOutput, calls=%fused_computation.10 | convolution fusion | flops 135397376 | bytes 3411968 | tf_op jit(solution)/shard_map/hrs,shd->rhd/dot_general | solution.py:68
  175.7 0.1 copy.16
  176.0 0.1 copy.15
  176.2 0.8 broadcast_select_fusion.5
  177.0 0.6 collective-permute-done.2
  177.5 0.7 copy.33
  (21 shorter events, 0.4 us)
Async XLA Ops:
  7.2 131.6 %copy-start = (s32[1,512]{1,0:T(1,128)S(1)}, s32[1,512]{1,0:T(1,128)}, u32[]{:S(2)}) copy-start(s32[1,512]{1,0:T(1,128)} %param.6) | copy-start | bytes 6148
  7.2 44.3 %all-gather.3.cloned.1.call-start = ((), (), s32[]{:S(2)}) async-start(), calls=%async_computation.4 | async-start | bytes 2129920 | tf_op jit(solution)/shard_map/all_gather | solution.py:83
  7.9 109.5 %reduce-scatter.3.cloned.1.call-start = ((), (), s32[]{:S(2)}) async-start(), calls=%async_computation.2 | async-start | bytes 5242880 | tf_op jit(solution)/shard_map/reduce_scatter | solution.py:95
  60.6 2.7 %copy-start.1 = (f32[512,3072]{1,0:T(8,128)}, f32[512,3072]{1,0:T(8,128)S(1)}, u32[]{:S(2)}) copy-start(f32[512,3072]{1,0:T(8,128)S(1)} %fusion.2) | copy-start | bytes 18874372
  65.8 104.5 %reduce-scatter.5.cloned.1.call-start = ((), (), s32[]{:S(2)}) async-start(), calls=%async_computation.3 | async-start | bytes 2621440 | tf_op jit(solution)/shard_map/reduce_scatter | solution.py:94
  117.4 19.8 %copy-start.2 = (f32[128,2048]{1,0:T(8,128)S(1)}, f32[128,2048]{1,0:T(8,128)}, u32[]{:S(2)}) copy-start(f32[128,2048]{1,0:T(8,128)} %reduce-scatter.3.cloned.1.call-done) | copy-start | bytes 3145732
  118.8 18.4 %collective-permute-start = (bf16[1,128,2048]{2,1,0:T(8,128)(2,1)S(1)}, bf16[1,128,2048]{2,1,0:T(8,128)(2,1)S(1)}, u32[]{:S(2)}, u32[]{:S(2)}) collective-permute-start(bf16[1,128,2048]{2,1,0:T(8,128)(2,1)S(1)} %convert_bitcast_fusion), channel_id=1, source_target_pairs={{0,1},{1,0},{2,3},{3,2},{4,5},{5,4},{6,7},{7,6},{8,9},{9,8},{10,11... | collective-permute-start | bytes 1572872 | tf_op jit(solution)/shard_map/ppermute | solution.py:26
  137.3 6.3 %copy-start.3 = (s32[1,4]{1,0:T(1,128)S(1)}, s32[1,4]{1,0:T(1,128)}, u32[]{:S(2)}) copy-start(s32[1,4]{1,0:T(1,128)} %param.7) | copy-start | bytes 52
  137.4 31.2 %collective-permute-start.1 = (bf16[2,128,2048]{2,1,0:T(8,128)(2,1)S(1)}, bf16[2,128,2048]{2,1,0:T(8,128)(2,1)S(1)}, u32[]{:S(2)}, u32[]{:S(2)}) collective-permute-start(bf16[2,128,2048]{2,1,0:T(8,128)(2,1)S(1)} %pad_maximum_fusion.1), channel_id=1, source_target_pairs={{0,2},{1,3},{2,0},{3,1},{4,6},{5,7},{6,4},{7,5},{8,10},{9,11},{10,... | collective-permute-start | bytes 3145736 | tf_op jit(solution)/shard_map/ppermute | solution.py:26
  175.9 1.6 collective-permute-start.2
Sparse Core Ops, SparseCore 0:
  9.6 41.8 all-gather.2
  65.9 51.4 reduce-scatter.2
  120.3 45.0 reduce-scatter.4
